TPU v7x, 256 devices: a whole 4x4x8 slice. The times are simulated.
256 devices in a mesh: row: 32 (over z, y), col: 8 (over x, core).
Axes of the slice: x: 4, y: 4, z: 8, core: 2. Of those that a mesh axis runs over, the one named last changes fastest.
Arguments:
- obstacles: float32 [3, 16384], P(None, 'row'), may hold values from 0 to 16
- particles: float32 [3, 8192], P(None, 'row'), may hold values from 0 to 16
- forces: float32 [3, 32, 8192], P(None, None, 'row'), may hold values from -0.8 to 0.8
- neighbours: int32 [64, 32], P('row', 'col'), may hold values from 0 to 127, as said below
- carried: float32 [128, 3, 32, 128], P('row'), may hold values from -6 to 6
- factor: float32 [2, 4096, 128, 3, 128], P(None, 'col', 'row'), may hold values from -0.09375 to 0.09375
- inverses: float32 [2, 4096, 4096], P(None, 'row', 'col'), may hold values from -0.09375 to 0.09375
Outputs:
- solved: float32 [2, 32, 4096], P(None, None, 'col')
- remaining: float32 [128, 3, 32, 128], P('row', None, 'col')
Inputs may be any that keep to these rules, and one draw needn't show every extreme that they name: `neighbours`: each particle block lists 32 different obstacle blocks, and every obstacle block is listed by exactly 16 particle blocks.
All inputs are finite; a program needn't handle non-finite values.
Results may differ from a plain program's by a relative error of at most 0.0001.
Values sent between devices are 32-bit elements; how exact they have to be, the bound alone decides.
No kernel may reach another device: no remote copies, remote signals or barrier semaphores. Data moves between devices by JAX's collectives and lax.ppermute only.
A program may use at most 64 MiB of HBM per device.

v0:
```python
import jax
import jax.numpy as jnp
from jax import lax
from jax.sharding import PartitionSpec as P

PANEL = 4096
BLOCK_PTS = 128
GROUP = 128
soften_square = 1.0
highest = lax.Precision.HIGHEST


def stokeslet(targets, sources, pushes, weight):
    difference = targets[:, :, None] - sources[:, None, :]
    radius = jnp.sum(difference * difference, axis=0) + soften_square
    inverse_cube = lax.rsqrt(radius) / radius * weight
    isotropic = (radius + soften_square) * inverse_cube
    speeds = []
    for left_comp in range(3):
        summed = jnp.einsum("sq,xq->sx", pushes[left_comp], isotropic, precision=highest)
        for right_comp in range(3):
            coupling = difference[left_comp] * difference[right_comp] * inverse_cube
            summed = summed + jnp.einsum(
                "sq,xq->sx", pushes[right_comp], coupling, precision=highest
            )
        speeds.append(summed)
    return jnp.stack(speeds)


def keep_mask(panel_step, block_count, diag_count):
    component = jnp.arange(3, dtype=jnp.int32)[None, :, None, None]
    position = (
        jnp.arange(block_count, dtype=jnp.int32)[:, None] * BLOCK_PTS
        + jnp.arange(BLOCK_PTS, dtype=jnp.int32)[None, :]
    )
    position = position[:, None, None, :]
    hidden_rows = (component <= panel_step) & (position < diag_count)
    return jnp.where(hidden_rows, 0.0, 1.0).astype(jnp.float32)


def diag_view(values, component, diag_count):
    picked = values[:, component]
    return picked.transpose(1, 0, 2).reshape(picked.shape[1], -1)[:, :diag_count]


def solve_block(diag_rows, inverse):
    partial_rows = jnp.dot(
        diag_rows, inverse, precision=highest, preferred_element_type=jnp.float32
    )
    return lax.psum(partial_rows, "row")


def panel_change(answer, panel_cols):
    return jnp.einsum("sj,jbai->basi", answer, panel_cols, precision=highest)


def body(obstacles, particles, forces, neighbours, carried, factor, inverses):
    row_count = lax.axis_size("row")
    col_count = lax.axis_size("col")
    block_count = obstacles.shape[1] // BLOCK_PTS
    diag_count = PANEL // row_count
    rhs_count = forces.shape[1]
    group_count = particles.shape[1] // GROUP
    rhs_share = rhs_count // col_count
    every_point = lax.all_gather(obstacles, "row", axis=1, tiled=True)
    point_blocks = every_point.reshape(3, -1, BLOCK_PTS)
    sources = particles.reshape(3, group_count, GROUP).transpose(1, 0, 2)
    pushes = forces.reshape(3, rhs_count, group_count, GROUP).transpose(2, 0, 1, 3)
    targets = point_blocks[:, neighbours].transpose(1, 2, 0, 3)
    pair_speed = jax.vmap(jax.vmap(stokeslet, (0, None, None, None)), (0, 0, 0, None))
    speeds = pair_speed(targets, sources, pushes, jnp.float32(1.0)).reshape(
        -1, 3, rhs_count, BLOCK_PTS
    )
    target_block = neighbours.reshape(-1)
    wanted = jnp.arange(block_count * lax.axis_size("row"), dtype=jnp.int32)
    onehot = (wanted[:, None] == target_block[None, :]).astype(jnp.float32)
    stokes_part = lax.psum_scatter(
        jnp.einsum("cp,pasi->casi", onehot, speeds, precision=highest),
        "row",
        scatter_dimension=0,
        tiled=True,
    )
    rhs_field = carried + lax.psum(stokes_part, "col")
    answers = []
    for panel_step in range(2):
        answer = solve_block(diag_view(rhs_field, panel_step, diag_count), inverses[panel_step])
        answers.append(answer)
        change = panel_change(answer, factor[panel_step]) * keep_mask(
            panel_step, block_count, diag_count
        )
        rhs_field = rhs_field - lax.psum(change, "col")
    remaining = lax.dynamic_slice_in_dim(rhs_field, lax.axis_index("col") * rhs_share, rhs_share, 2)
    return (jnp.stack(answers), remaining)


def solution(mesh):
    in_specs = (
        P(None, "row"),
        P(None, "row"),
        P(None, None, "row"),
        P("row", "col"),
        P("row", None, None, None),
        P(None, "col", "row", None, None),
        P(None, "row", "col"),
    )
    out_specs = (P(None, None, "col"), P("row", None, "col", None))
    return jax.shard_map(body, mesh=mesh, in_specs=in_specs, out_specs=out_specs, check_vma=False)
```

profile of v0, /device:TPU:8, one launch (start us, length us, event | category | flops | bytes accessed | tf_op | source)
XLA Modules:
  0.0 803.6 jit_solution(12957455357524606495)
XLA Ops:
  7.2 0.0 reduce-scatter.2.cloned.1.call-start
  7.2 52.1 %all_gather.3 = f32[3,16384]{1,0:T(4,128)S(1)} all-gather(f32[3,512]{1,0:T(4,128)} %param.7), channel_id=1, replica_groups=mesh['row'=32,'col'=8] {'row'}, dimensions={1}, use_global_device_ids=true | all-gather | bytes 202752 | tf_op jit(solution)/shard_map/all_gather | solution.py:65
  59.3 0.7 compare_select_fusion
  60.0 0.1 reshape.87
  60.1 0.6 gather_fusion
  60.7 0.7 reshape.80
  61.4 0.5 broadcast_subtract_fusion
  61.9 0.7 fusion.25
  62.6 0.7 fusion.26
  63.4 0.7 fusion.27
  64.2 0.1 eq.16
  64.2 0.7 convolution_add_fusion.8
  65.0 0.7 convolution_add_fusion.7
  65.7 0.7 fusion.8
  66.5 0.7 convolution_add_fusion.5
  67.2 0.7 convolution_add_fusion.4
  68.0 0.7 fusion.7
  68.7 0.7 convolution_add_fusion.2
  69.5 0.7 convolution_add_fusion.1
  70.2 0.7 fusion.6
  71.0 2.7 fusion.15
  73.7 6.5 copy.34
  80.2 0.0 reduce-scatter.2.cloned.1.call-update
  80.2 0.0 all-reduce.6.cloned.1.call-start
  80.3 0.1 add_compare_fusion
  80.4 5.6 fusion.33
  86.0 218.5 %reduce-scatter.2.cloned.1.call-done = f32[4,3,32,128]{3,2,1,0:T(8,128)} async-done(((f32[128,3,32,128]{3,2,1,0:T(8,128)}), f32[4,3,32,128]{3,2,1,0:T(8,128)}) %reduce-scatter.2.cloned.1.call-update) | async-done | bytes 196624 | tf_op jit(solution)/shard_map/reduce_scatter | solution.py:77
  304.6 0.0 all-reduce.8.cloned.1.call-start
  304.6 66.6 %all-reduce.6.cloned.1.call-done = f32[4,3,32,128]{3,2,1,0:T(8,128)} async-done(((f32[4,3,32,128]{3,2,1,0:T(8,128)}), f32[4,3,32,128]{3,2,1,0:T(8,128)}) %all-reduce.6.cloned.1.call-update) | async-done | bytes 196624 | tf_op jit(solution)/shard_map/psum | solution.py:83
  371.2 1.0 add.119
  372.3 1.8 fusion.19
  374.1 0.0 all-reduce.8.cloned.1.call-update
  374.1 0.0 all-reduce.10.cloned.1.call-start
  374.2 0.1 and_select_fusion
  374.2 141.4 %all-reduce.8.cloned.1.call-done = f32[32,512]{1,0:T(8,128)} async-done(((f32[32,512]{1,0:T(8,128)}), f32[32,512]{1,0:T(8,128)}) %all-reduce.8.cloned.1.call-update) | async-done | bytes 65552 | tf_op jit(solution)/shard_map/psum | solution.py:50
  515.7 4.5 fusion.3
  520.2 0.0 all-reduce.12.cloned.1.call-start
  520.2 63.6 %all-reduce.10.cloned.1.call-done = f32[4,3,32,128]{3,2,1,0:T(8,128)} async-done(((f32[4,3,32,128]{3,2,1,0:T(8,128)}), f32[4,3,32,128]{3,2,1,0:T(8,128)}) %all-reduce.10.cloned.1.call-update) | async-done | bytes 196624 | tf_op jit(solution)/shard_map/psum | solution.py:91
  583.8 1.0 sub.22
  584.8 0.7 copy-done.1
  585.4 1.8 fusion.17
  587.3 0.0 all-reduce.12.cloned.1.call-update
  587.3 0.0 all-reduce.14.cloned.1.call-start
  587.3 140.8 %all-reduce.12.cloned.1.call-done = f32[32,512]{1,0:T(8,128)} async-done(((f32[32,512]{1,0:T(8,128)}), f32[32,512]{1,0:T(8,128)}) %all-reduce.12.cloned.1.call-update) | async-done | bytes 65552 | tf_op jit(solution)/shard_map/psum | solution.py:50
  728.2 3.5 fusion.5
  731.7 0.7 pad_maximum_fusion.1
  732.4 62.9 %all-reduce.14.cloned.1.call-done = f32[4,3,32,128]{3,2,1,0:T(8,128)} async-done(((f32[4,3,32,128]{3,2,1,0:T(8,128)}), f32[4,3,32,128]{3,2,1,0:T(8,128)}) %all-reduce.14.cloned.1.call-update) | async-done | bytes 196624 | tf_op jit(solution)/shard_map/psum | solution.py:91
  795.3 1.4 dynamic-slice_subtract_fusion
  (20 shorter events, 0.1 us)
Async XLA Ops:
  7.2 54.2 %copy-start = (f32[3,32,256]{2,1,0:T(8,128)S(1)}, f32[3,32,256]{2,1,0:T(8,128)}, u32[]{:S(2)}) copy-start(f32[3,32,256]{2,1,0:T(8,128)} %param.9) | copy-start | bytes 294916
  7.2 297.4 %reduce-scatter.2.cloned.1.call-start = ((), (), s32[]{:S(2)}) async-start(), calls=%async_computation.1 | async-start | bytes 6488064 | tf_op jit(solution)/shard_map/reduce_scatter | solution.py:77
  63.4 0.8 copy-start.4
  80.2 291.0 %all-reduce.6.cloned.1.call-start = ((), (), s32[]{:S(2)}) async-start(), calls=%async_computation.2 | async-start | bytes 393216 | tf_op jit(solution)/shard_map/psum | solution.py:83
  304.6 211.1 %all-reduce.8.cloned.1.call-start = ((), (), s32[]{:S(2)}) async-start(), calls=%async_computation.3 | async-start | bytes 131072 | tf_op jit(solution)/shard_map/psum | solution.py:50
  374.1 209.7 %all-reduce.10.cloned.1.call-start = ((), (), s32[]{:S(2)}) async-start(), calls=%async_computation.4 | async-start | bytes 393216 | tf_op jit(solution)/shard_map/psum | solution.py:91
  520.2 208.0 %all-reduce.12.cloned.1.call-start = ((), (), s32[]{:S(2)}) async-start(), calls=%async_computation.5 | async-start | bytes 131072 | tf_op jit(solution)/shard_map/psum | solution.py:50
  584.8 0.7 copy-start.1
  587.3 208.0 %all-reduce.14.cloned.1.call-start = ((), (), s32[]{:S(2)}) async-start(), calls=%async_computation.6 | async-start | bytes 393216 | tf_op jit(solution)/shard_map/psum | solution.py:91
  728.2 3.5 copy-start.2
  728.2 3.5 copy-start.3
Sparse Core Ops, SparseCore 0:
  80.4 224.1 reduce-scatter.1
  306.8 64.3 all-reduce.5
  375.2 140.3 all-reduce.7
  520.3 63.4 all-reduce.9
  587.7 140.4 all-reduce.11
  731.8 63.4 all-reduce.13
where the time goes:
time: 804 us
  waiting for transfers between devices  694 us (86%)
  blocking collectives  52.1 us (6%)
  matrix products  23.3 us (3%)
  local copies, waits for them, and re-layouts  14.3 us (2%)
  between operations  14.3 us (2%)
    psum x2, waiting for transfers between devices, solve_block(): return lax.psum(partial_rows, 'row')  282 us
    reduce_scatter x1, waiting for transfers between devices, body(): lax.psum_scatter(jnp.einsum('cp,pasi->casi', onehot, speeds, precision=hi...  219 us
    psum x2, waiting for transfers between devices, body(): rhs_field = rhs_field - lax.psum(change, 'col')  127 us
    psum x1, waiting for transfers between devices, body(): rhs_field = carried + lax.psum(stokes_part, 'col')  66.6 us
    all_gather x1, blocking collectives, body(): every_point = lax.all_gather(obstacles, 'row', axis=1, tiled=True)  52.1 us
  transfers between devices with their start and end apart: 6, of which 6 were waited for; matrix products, arithmetic and copies ran while one was open for 1% of the time, Pallas kernels for 0%

commit v1 on v0

--- a/solution.py
+++ b/solution.py
@@ -80,7 +80,7 @@
         scatter_dimension=0,
         tiled=True,
     )
-    rhs_field = carried + lax.psum(stokes_part, "col")
+    rhs_field = carried + jnp.sum(lax.all_gather(stokes_part, "col"), axis=0)
     answers = []
     for panel_step in range(2):
         answer = solve_block(diag_view(rhs_field, panel_step, diag_count), inverses[panel_step])

time: 804 us -> 767 us (0.954)
  waiting for transfers between devices: 694 us -> 655 us
    psum x1 -> x0, waiting for transfers between devices: 66.6 us -> none  [body(): rhs_field = carried + lax.psum(stokes_part, 'col')]
    all_gather x0 -> x1, waiting for transfers between devices: none -> 22 us  [body(): rhs_field = carried + jnp.sum(lax.all_gather(stokes_part, 'col'), axis=0)]
where the time goes in v1:
time: 767 us
  waiting for transfers between devices  655 us (85%)
  blocking collectives  52.1 us (7%)
  matrix products  23.3 us (3%)
  between operations  14.3 us (2%)
  local copies, waits for them, and re-layouts  14.2 us (2%)
  other arithmetic  7.7 us (1%)
    psum x2, waiting for transfers between devices, solve_block(): return lax.psum(partial_rows, 'row')  282 us
    reduce_scatter x1, waiting for transfers between devices, body(): lax.psum_scatter(jnp.einsum('cp,pasi->casi', onehot, speeds, precision=hi...  224 us
    psum x2, waiting for transfers between devices, body(): rhs_field = rhs_field - lax.psum(change, 'col')  127 us
    all_gather x1, blocking collectives, body(): every_point = lax.all_gather(obstacles, 'row', axis=1, tiled=True)  52.1 us
    all_gather x1, waiting for transfers between devices, body(): rhs_field = carried + jnp.sum(lax.all_gather(stokes_part, 'col'), axis=0)  22 us
  transfers between devices with their start and end apart: 6, of which 6 were waited for; matrix products, arithmetic and copies ran while one was open for 1% of the time, Pallas kernels for 0%

profile of v1, /device:TPU:8, one launch (start us, length us, event | category | flops | bytes accessed | tf_op | source)
XLA Modules:
  0.0 767.0 jit_solution(5038619923983564010)
XLA Ops:
  7.2 0.0 reduce-scatter.2.cloned.1.call-start
  7.2 52.1 %all_gather.9 = f32[3,16384]{1,0:T(4,128)S(1)} all-gather(f32[3,512]{1,0:T(4,128)} %param.7), channel_id=1, replica_groups=mesh['row'=32,'col'=8] {'row'}, dimensions={1}, use_global_device_ids=true | all-gather | bytes 202752 | tf_op jit(solution)/shard_map/all_gather | solution.py:65
  59.3 0.7 compare_select_fusion
  60.0 0.1 reshape.87
  60.1 0.6 gather_fusion
  60.7 0.7 reshape.80
  61.4 0.5 broadcast_subtract_fusion
  61.9 0.7 fusion.25
  62.6 0.7 fusion.26
  63.4 0.7 fusion.27
  64.2 0.1 eq.16
  64.2 0.7 convolution_add_fusion.8
  65.0 0.7 convolution_add_fusion.7
  65.7 0.7 fusion.8
  66.5 0.7 convolution_add_fusion.5
  67.2 0.7 convolution_add_fusion.4
  68.0 0.7 fusion.7
  68.7 0.7 convolution_add_fusion.2
  69.5 0.7 convolution_add_fusion.1
  70.2 0.7 fusion.6
  71.0 2.7 fusion.15
  73.7 6.5 copy.22
  80.2 0.0 reduce-scatter.2.cloned.1.call-update
  80.2 0.0 all-gather.3.cloned.1.call-start
  80.3 224.2 %reduce-scatter.2.cloned.1.call-done = f32[4,3,32,128]{3,2,1,0:T(8,128)} async-done(((f32[128,3,32,128]{3,2,1,0:T(8,128)}), f32[4,3,32,128]{3,2,1,0:T(8,128)}) %reduce-scatter.2.cloned.1.call-update) | async-done | bytes 196624 | tf_op jit(solution)/shard_map/reduce_scatter | solution.py:77
  304.6 0.0 all-reduce.5.cloned.1.call-start
  304.6 0.1 add_compare_fusion
  304.7 5.6 fusion.33
  310.3 22.0 %all-gather.3.cloned.1.call-done = f32[32,3,32,128]{3,2,1,0:T(8,128)} async-done(((f32[4,3,32,128]{3,2,1,0:T(8,128)}), f32[32,3,32,128]{3,2,1,0:T(8,128)}) %all-gather.3.cloned.1.call-update) | async-done | bytes 1572880 | tf_op jit(solution)/shard_map/all_gather | solution.py:83
  332.3 2.2 reduce_sum.19
  334.5 1.0 add.117
  335.6 1.8 fusion.19
  337.4 0.0 all-reduce.5.cloned.1.call-update
  337.4 0.0 all-reduce.7.cloned.1.call-start
  337.5 0.1 and_select_fusion
  337.6 141.5 %all-reduce.5.cloned.1.call-done = f32[32,512]{1,0:T(8,128)} async-done(((f32[32,512]{1,0:T(8,128)}), f32[32,512]{1,0:T(8,128)}) %all-reduce.5.cloned.1.call-update) | async-done | bytes 65552 | tf_op jit(solution)/shard_map/psum | solution.py:50
  479.0 4.5 fusion.3
  483.6 0.0 all-reduce.9.cloned.1.call-start
  483.6 63.6 %all-reduce.7.cloned.1.call-done = f32[4,3,32,128]{3,2,1,0:T(8,128)} async-done(((f32[4,3,32,128]{3,2,1,0:T(8,128)}), f32[4,3,32,128]{3,2,1,0:T(8,128)}) %all-reduce.7.cloned.1.call-update) | async-done | bytes 196624 | tf_op jit(solution)/shard_map/psum | solution.py:91
  547.2 1.0 sub.22
  548.2 0.7 copy-done.1
  548.8 1.8 fusion.17
  550.7 0.0 all-reduce.11.cloned.1.call-start
  550.7 140.8 %all-reduce.9.cloned.1.call-done = f32[32,512]{1,0:T(8,128)} async-done(((f32[32,512]{1,0:T(8,128)}), f32[32,512]{1,0:T(8,128)}) %all-reduce.9.cloned.1.call-update) | async-done | bytes 65552 | tf_op jit(solution)/shard_map/psum | solution.py:50
  691.6 3.5 fusion.5
  695.1 0.7 pad_maximum_fusion.1
  695.8 62.9 %all-reduce.11.cloned.1.call-done = f32[4,3,32,128]{3,2,1,0:T(8,128)} async-done(((f32[4,3,32,128]{3,2,1,0:T(8,128)}), f32[4,3,32,128]{3,2,1,0:T(8,128)}) %all-reduce.11.cloned.1.call-update) | async-done | bytes 196624 | tf_op jit(solution)/shard_map/psum | solution.py:91
  758.7 1.4 dynamic-slice_subtract_fusion
  (21 shorter events, 0.2 us)
Async XLA Ops:
  7.2 54.2 %copy-start = (f32[3,32,256]{2,1,0:T(8,128)S(1)}, f32[3,32,256]{2,1,0:T(8,128)}, u32[]{:S(2)}) copy-start(f32[3,32,256]{2,1,0:T(8,128)} %param.9) | copy-start | bytes 294916
  7.2 297.4 %reduce-scatter.2.cloned.1.call-start = ((), (), s32[]{:S(2)}) async-start(), calls=%async_computation.1 | async-start | bytes 6488064 | tf_op jit(solution)/shard_map/reduce_scatter | solution.py:77
  63.4 0.8 copy-start.4
  80.2 252.0 %all-gather.3.cloned.1.call-start = ((), (), s32[]{:S(2)}) async-start(), calls=%async_computation.6 | async-start | bytes 1769472 | tf_op jit(solution)/shard_map/all_gather | solution.py:83
  304.6 174.5 %all-reduce.5.cloned.1.call-start = ((), (), s32[]{:S(2)}) async-start(), calls=%async_computation.2 | async-start | bytes 131072 | tf_op jit(solution)/shard_map/psum | solution.py:50
  337.4 209.8 %all-reduce.7.cloned.1.call-start = ((), (), s32[]{:S(2)}) async-start(), calls=%async_computation.3 | async-start | bytes 393216 | tf_op jit(solution)/shard_map/psum | solution.py:91
  483.6 208.0 %all-reduce.9.cloned.1.call-start = ((), (), s32[]{:S(2)}) async-start(), calls=%async_computation.4 | async-start | bytes 131072 | tf_op jit(solution)/shard_map/psum | solution.py:50
  548.2 0.7 copy-start.1
  550.7 208.0 %all-reduce.11.cloned.1.call-start = ((), (), s32[]{:S(2)}) async-start(), calls=%async_computation.5 | async-start | bytes 393216 | tf_op jit(solution)/shard_map/psum | solution.py:91
  691.6 3.5 copy-start.2
  691.6 3.5 copy-start.3
Sparse Core Ops, SparseCore 0:
  80.4 224.1 reduce-scatter.1
  306.4 25.8 all-gather.2
  337.5 141.4 all-reduce.4
  483.7 63.4 all-reduce.6
  551.1 140.4 all-reduce.8
  695.2 63.4 all-reduce.10

commit v2 on v0

--- a/solution.py
+++ b/solution.py
@@ -62,7 +62,9 @@
     rhs_count = forces.shape[1]
     group_count = particles.shape[1] // GROUP
     rhs_share = rhs_count // col_count
-    every_point = lax.all_gather(obstacles, "row", axis=1, tiled=True)
+    every_point = jnp.concatenate(
+        lax.all_to_all(jnp.stack([obstacles] * lax.axis_size("row")), "row", 0, 0), axis=1
+    )
     point_blocks = every_point.reshape(3, -1, BLOCK_PTS)
     sources = particles.reshape(3, group_count, GROUP).transpose(1, 0, 2)
     pushes = forces.reshape(3, rhs_count, group_count, GROUP).transpose(2, 0, 1, 3)

time: 804 us -> 773 us (0.961)
  blocking collectives: 52.1 us -> 0 us
  starting transfers between devices: 0.24 us -> 11.9 us
    all_gather x1 -> x0, blocking collectives: 52.1 us -> none  [body(): every_point = lax.all_gather(obstacles, 'row', axis=1, tiled=True)]
    all_to_all x0 -> x1, starting transfers between devices: none -> 11.7 us  [body(): lax.all_to_all(jnp.stack([obstacles] * lax.axis_size('row')), 'row', 0, 0)]
    all_to_all x0 -> x1, waiting for transfers between devices: none -> 8.91 us  [body(): lax.all_to_all(jnp.stack([obstacles] * lax.axis_size('row')), 'row', 0, 0)]
  transfers between devices with their start and end apart: 6 -> 7, of which waited for: 6 -> 7; matrix products, arithmetic and copies ran while one was open for 1% -> 1% of each run, Pallas kernels for 0% -> 0%
where the time goes in v2:
time: 773 us
  waiting for transfers between devices  701 us (91%)
  matrix products  23.3 us (3%)
  local copies, waits for them, and re-layouts  16.4 us (2%)
  between operations  14.3 us (2%)
  starting transfers between devices  11.9 us (2%)
    psum x2, waiting for transfers between devices, solve_block(): return lax.psum(partial_rows, 'row')  282 us
    reduce_scatter x1, waiting for transfers between devices, body(): lax.psum_scatter(jnp.einsum('cp,pasi->casi', onehot, speeds, precision=hi...  217 us
    psum x2, waiting for transfers between devices, body(): rhs_field = rhs_field - lax.psum(change, 'col')  127 us
    psum x1, waiting for transfers between devices, body(): rhs_field = carried + lax.psum(stokes_part, 'col')  66.5 us
  transfers between devices with their start and end apart: 7, of which 7 were waited for; matrix products, arithmetic and copies ran while one was open for 1% of the time, Pallas kernels for 0%

profile of v2, /device:TPU:8, one launch (start us, length us, event | category | flops | bytes accessed | tf_op | source)
XLA Modules:
  0.0 772.9 jit_solution(15008046514683930534)
XLA Ops:
  7.2 1.5 stack.16
  8.6 11.7 %all-to-all-start = ((f32[32,3,512]{2,1,0:T(4,128)}), f32[32,3,512]{2,1,0:T(4,128)S(1)}, u32[]{:S(2)}, u32[]{:S(2)}) async-start(f32[32,3,512]{2,1,0:T(4,128)} %stack.16), calls=%async_computation | async-start | bytes 524288 | tf_op jit(solution)/shard_map/all_to_all | solution.py:66
  20.3 0.0 reduce-scatter.2.cloned.1.call-start
  20.4 0.7 compare_select_fusion
  21.1 0.8 eq.16
  21.8 0.1 reshape.89
  21.9 0.7 reshape.82
  22.7 8.9 %all-to-all-done = f32[32,3,512]{2,1,0:T(4,128)S(1)} async-done(((f32[32,3,512]{2,1,0:T(4,128)}), f32[32,3,512]{2,1,0:T(4,128)S(1)}, u32[]{:S(2)}, u32[]{:S(2)}) %all-to-all-start) | async-done | bytes 196640 | tf_op jit(solution)/shard_map/all_to_all | solution.py:66
  31.6 0.6 gather_fusion
  32.1 0.5 broadcast_subtract_fusion
  32.6 0.7 fusion.25
  33.4 0.7 fusion.26
  34.1 0.7 fusion.27
  34.9 0.7 convolution_add_fusion.8
  35.6 0.7 convolution_add_fusion.7
  36.4 0.7 fusion.8
  37.1 0.7 convolution_add_fusion.5
  37.9 0.7 convolution_add_fusion.4
  38.6 0.7 fusion.7
  39.4 0.7 convolution_add_fusion.2
  40.1 0.7 convolution_add_fusion.1
  40.9 0.7 fusion.6
  41.7 2.7 fusion.15
  44.4 6.5 copy.39
  50.9 0.0 reduce-scatter.2.cloned.1.call-update
  50.9 0.0 all-reduce.6.cloned.1.call-start
  50.9 0.1 add_compare_fusion
  51.0 5.6 fusion.33
  56.6 217.2 %reduce-scatter.2.cloned.1.call-done = f32[4,3,32,128]{3,2,1,0:T(8,128)} async-done(((f32[128,3,32,128]{3,2,1,0:T(8,128)}), f32[4,3,32,128]{3,2,1,0:T(8,128)}) %reduce-scatter.2.cloned.1.call-update) | async-done | bytes 196624 | tf_op jit(solution)/shard_map/reduce_scatter | solution.py:79
  273.9 0.0 all-reduce.8.cloned.1.call-start
  273.9 66.5 %all-reduce.6.cloned.1.call-done = f32[4,3,32,128]{3,2,1,0:T(8,128)} async-done(((f32[4,3,32,128]{3,2,1,0:T(8,128)}), f32[4,3,32,128]{3,2,1,0:T(8,128)}) %all-reduce.6.cloned.1.call-update) | async-done | bytes 196624 | tf_op jit(solution)/shard_map/psum | solution.py:85
  340.5 1.0 add.119
  341.5 1.8 fusion.19
  343.4 0.0 all-reduce.10.cloned.1.call-start
  343.5 0.1 and_select_fusion
  343.5 141.4 %all-reduce.8.cloned.1.call-done = f32[32,512]{1,0:T(8,128)} async-done(((f32[32,512]{1,0:T(8,128)}), f32[32,512]{1,0:T(8,128)}) %all-reduce.8.cloned.1.call-update) | async-done | bytes 65552 | tf_op jit(solution)/shard_map/psum | solution.py:50
  484.9 4.5 fusion.3
  489.5 0.0 all-reduce.12.cloned.1.call-start
  489.5 63.6 %all-reduce.10.cloned.1.call-done = f32[4,3,32,128]{3,2,1,0:T(8,128)} async-done(((f32[4,3,32,128]{3,2,1,0:T(8,128)}), f32[4,3,32,128]{3,2,1,0:T(8,128)}) %all-reduce.10.cloned.1.call-update) | async-done | bytes 196624 | tf_op jit(solution)/shard_map/psum | solution.py:93
  553.1 1.0 sub.22
  554.1 0.7 copy-done.1
  554.7 1.8 fusion.17
  556.6 0.0 all-reduce.14.cloned.1.call-start
  556.6 140.8 %all-reduce.12.cloned.1.call-done = f32[32,512]{1,0:T(8,128)} async-done(((f32[32,512]{1,0:T(8,128)}), f32[32,512]{1,0:T(8,128)}) %all-reduce.12.cloned.1.call-update) | async-done | bytes 65552 | tf_op jit(solution)/shard_map/psum | solution.py:50
  697.5 3.5 fusion.5
  701.0 0.7 pad_maximum_fusion.1
  701.7 62.9 %all-reduce.14.cloned.1.call-done = f32[4,3,32,128]{3,2,1,0:T(8,128)} async-done(((f32[4,3,32,128]{3,2,1,0:T(8,128)}), f32[4,3,32,128]{3,2,1,0:T(8,128)}) %all-reduce.14.cloned.1.call-update) | async-done | bytes 196624 | tf_op jit(solution)/shard_map/psum | solution.py:93
  764.6 1.4 dynamic-slice_subtract_fusion
  (20 shorter events, 0.2 us)
Async XLA Ops:
  7.2 15.5 %copy-start = (f32[3,32,256]{2,1,0:T(8,128)S(1)}, f32[3,32,256]{2,1,0:T(8,128)}, u32[]{:S(2)}) copy-start(f32[3,32,256]{2,1,0:T(8,128)} %param.9) | copy-start | bytes 294916
  8.6 22.9 %all-to-all-start = ((f32[32,3,512]{2,1,0:T(4,128)}), f32[32,3,512]{2,1,0:T(4,128)S(1)}, u32[]{:S(2)}, u32[]{:S(2)}) async-start(f32[32,3,512]{2,1,0:T(4,128)} %stack.16), calls=%async_computation | async-start | bytes 524288 | tf_op jit(solution)/shard_map/all_to_all | solution.py:66
  20.3 253.5 %reduce-scatter.2.cloned.1.call-start = ((), (), s32[]{:S(2)}) async-start(), calls=%async_computation.2 | async-start | bytes 6488064 | tf_op jit(solution)/shard_map/reduce_scatter | solution.py:79
  50.9 289.6 %all-reduce.6.cloned.1.call-start = ((), (), s32[]{:S(2)}) async-start(), calls=%async_computation.3 | async-start | bytes 393216 | tf_op jit(solution)/shard_map/psum | solution.py:85
  273.9 211.1 %all-reduce.8.cloned.1.call-start = ((), (), s32[]{:S(2)}) async-start(), calls=%async_computation.4 | async-start | bytes 131072 | tf_op jit(solution)/shard_map/psum | solution.py:50
  343.4 209.7 %all-reduce.10.cloned.1.call-start = ((), (), s32[]{:S(2)}) async-start(), calls=%async_computation.5 | async-start | bytes 393216 | tf_op jit(solution)/shard_map/psum | solution.py:93
  489.5 208.0 %all-reduce.12.cloned.1.call-start = ((), (), s32[]{:S(2)}) async-start(), calls=%async_computation.6 | async-start | bytes 131072 | tf_op jit(solution)/shard_map/psum | solution.py:50
  554.0 0.7 copy-start.1
  556.6 208.0 %all-reduce.14.cloned.1.call-start = ((), (), s32[]{:S(2)}) async-start(), calls=%async_computation.7 | async-start | bytes 393216 | tf_op jit(solution)/shard_map/psum | solution.py:93
  697.4 3.5 copy-start.2
  697.4 3.5 copy-start.3
Sparse Core Ops, SparseCore 0:
  51.0 222.8 reduce-scatter.1
  276.2 64.2 all-reduce.5
  344.5 140.3 all-reduce.7
  489.6 63.4 all-reduce.9
  557.0 140.4 all-reduce.11
  701.1 63.4 all-reduce.13
